TPU v7x, 32 devices: a whole 2x2x4 slice. The times are simulated.
32 devices in a mesh: tm: 2 (over x), cell: 16 (over z, y, core).
Axes of the slice: x: 2, y: 2, z: 4, core: 2. Of those that a mesh axis runs over, the one named last changes fastest.
Arguments:
- initial: float32 [4096, 128], P('cell'), may hold values from 0.2 to 6, as said below
- source: float32 [4, 4096, 128], P('tm', 'cell'), may hold values from -1.8 to 1.8
- mix_rate: float32 [128], replicated, may hold values from 0.05 to 0.4
- fine_inverse: float32 [4, 32, 128, 128], P('tm', 'cell'), may hold values from -0.1 to 0.9, as said below
- coarse_inverse: float32 [4, 32, 128, 128], P('tm', 'cell'), may hold values from -0.1 to 1, as said below
- step_counts: int32 [4096], P('cell'), may hold values from 4 to 8
Outputs:
- finals: float32 [4, 4096, 128], P('tm', 'cell')
Inputs may be any that keep to these rules, and one draw needn't show every extreme that they name: `initial`: positive compositions. `fine_inverse`: each matrix is a positive diagonal plus small off-diagonal entries. `coarse_inverse`: each matrix is a positive diagonal plus small off-diagonal entries.
All inputs are finite; a program needn't handle non-finite values.
Results may differ from a plain program's by a relative error of at most 0.00011.
Values sent between devices are 32-bit elements; how exact they have to be, the bound alone decides.
No kernel may reach another device: no remote copies, remote signals or barrier semaphores. Data moves between devices by JAX's collectives and lax.ppermute only.
A program may use at most 64 MiB of HBM per device.

v0:
```python
import jax
import jax.numpy as jnp
from jax import lax
from jax.sharding import PartitionSpec as P

FINE_MAX = 8
ITERS = 2


def from_behind(block, axis, distance):
    devices = range(lax.axis_size(axis))
    route = [(i - distance, i) for i in devices if i - distance in devices]
    return lax.ppermute(block, axis, route)


def group_mul(state, matrices):
    count, width = state.shape
    groups = matrices.shape[0]
    shaped = state.reshape(groups, count // groups, width)
    result = jnp.einsum("gcs,gst->gct", shaped, matrices, precision=lax.Precision.HIGHEST)
    return result.reshape(count, width)


def slices_mul(state, matrices):
    lead, count, width = state.shape
    groups = matrices.shape[1]
    shaped = state.reshape(lead, groups, count // groups, width)
    result = jnp.einsum("lgcs,lgst->lgct", shaped, matrices, precision=lax.Precision.HIGHEST)
    return result.reshape(lead, count, width)


def local_chain(incoming, offsets, coarse_inverse):
    state = incoming
    results = []
    for index in range(offsets.shape[0]):
        state = group_mul(state, coarse_inverse[index]) + offsets[index]
        results.append(state)
    return jnp.stack(results, axis=0)


def zero_start_end(offsets, coarse_inverse):
    state = offsets[0]
    state = group_mul(state, coarse_inverse[1]) + offsets[1]
    return state


def across(initial, offsets, coarse_inverse):
    composed = coarse_inverse[0]
    composed = jnp.einsum(
        "gst,gtu->gsu", composed, coarse_inverse[1], precision=lax.Precision.HIGHEST
    )
    shifted = zero_start_end(offsets, coarse_inverse)
    leading = lax.axis_index("tm") == 0

    def advance(turn, incoming):
        ending = group_mul(incoming, composed) + shifted
        received = from_behind(ending, "tm", 1)
        return jnp.where(leading, initial, received)

    incoming = lax.fori_loop(0, lax.axis_size("tm") - 1, advance, initial)
    return (incoming, local_chain(incoming, offsets, coarse_inverse))


def body(initial, source, mix_rate, fine_inverse, coarse_inverse, step_counts):
    total = initial.shape[0] * lax.axis_size("cell")
    offsets0 = slices_mul(source, coarse_inverse)
    incoming, finals = across(initial, offsets0, coarse_inverse)
    for sweep_round in range(ITERS):
        starts = jnp.concatenate([incoming[None], finals[:-1]], axis=0)
        state = starts
        for substep in range(FINE_MAX):
            average = lax.psum(jnp.sum(state, axis=1), "cell") / total
            moved = slices_mul(
                state + source + mix_rate * (average[:, None, :] - state), fine_inverse
            )
            active = (substep < step_counts)[None, :, None]
            state = jnp.where(active, moved, state)
        coarse_ends = slices_mul(starts, coarse_inverse) + offsets0
        offsets = offsets0 + state - coarse_ends
        incoming, finals = across(initial, offsets, coarse_inverse)
    return finals


def solution(mesh):
    return jax.shard_map(
        body,
        mesh=mesh,
        in_specs=(
            P("cell", None),
            P("tm", "cell", None),
            P(),
            P("tm", "cell", None, None),
            P("tm", "cell", None, None),
            P("cell"),
        ),
        out_specs=P("tm", "cell", None),
        check_vma=False,
    )
```

profile of v0, /device:TPU:0, one launch (start us, length us, event | category | flops | bytes accessed | tf_op | source)
XLA Modules:
  0.0 515.5 jit_solution(2411006129935054928)
XLA Ops:
  0.0 1.5 fusion.61
  1.5 0.7 copy-done.3
  3.1 0.6 copy-done.5
  4.0 0.6 slice-done
  4.6 4.9 collective-permute-start
  9.5 0.7 copy-done.7
  10.2 2.0 collective-permute-done
  12.6 0.7 copy-done.4
  13.3 32.6 %psum.112 = f32[2,128]{1,0:T(2,128)S(1)} all-reduce(f32[2,128]{1,0:T(2,128)S(1)} %fusion.9), channel_id=1, replica_groups=mesh['tm'=2,'cell'=16] {'cell'}, use_global_device_ids=true, to_apply=%region_1.2 | all-reduce | flops 256 | bytes 2048 | tf_op jit(solution)/shard_map/psum | solution.py:72
  46.4 0.5 copy-done.1
  47.4 29.5 %psum.113 = f32[2,128]{1,0:T(2,128)S(1)} all-reduce(f32[2,128]{1,0:T(2,128)S(1)} %get-tuple-element.85), channel_id=1, replica_groups=mesh['tm'=2,'cell'=16] {'cell'}, use_global_device_ids=true, to_apply=%region_3.4 | all-reduce | flops 256 | bytes 2048 | tf_op jit(solution)/shard_map/psum | solution.py:72
  77.4 29.5 %psum.114 = f32[2,128]{1,0:T(2,128)S(1)} all-reduce(f32[2,128]{1,0:T(2,128)S(1)} %get-tuple-element.100), channel_id=1, replica_groups=mesh['tm'=2,'cell'=16] {'cell'}, use_global_device_ids=true, to_apply=%region_5.6 | all-reduce | flops 256 | bytes 2048 | tf_op jit(solution)/shard_map/psum | solution.py:72
  107.1 0.4 fusion.56
  107.5 29.5 %psum.115 = f32[2,128]{1,0:T(2,128)S(1)} all-reduce(f32[2,128]{1,0:T(2,128)S(1)} %get-tuple-element.81), channel_id=1, replica_groups=mesh['tm'=2,'cell'=16] {'cell'}, use_global_device_ids=true, to_apply=%region_7.8 | all-reduce | flops 256 | bytes 2048 | tf_op jit(solution)/shard_map/psum | solution.py:72
  137.6 29.5 %psum.116 = f32[2,128]{1,0:T(2,128)S(1)} all-reduce(f32[2,128]{1,0:T(2,128)S(1)} %get-tuple-element.103), channel_id=1, replica_groups=mesh['tm'=2,'cell'=16] {'cell'}, use_global_device_ids=true, to_apply=%region_9.10 | all-reduce | flops 256 | bytes 2048 | tf_op jit(solution)/shard_map/psum | solution.py:72
  167.6 29.5 %psum.117 = f32[2,128]{1,0:T(2,128)S(1)} all-reduce(f32[2,128]{1,0:T(2,128)S(1)} %get-tuple-element.77), channel_id=1, replica_groups=mesh['tm'=2,'cell'=16] {'cell'}, use_global_device_ids=true, to_apply=%region_11.12 | all-reduce | flops 256 | bytes 2048 | tf_op jit(solution)/shard_map/psum | solution.py:72
  197.7 29.5 %psum.118 = f32[2,128]{1,0:T(2,128)S(1)} all-reduce(f32[2,128]{1,0:T(2,128)S(1)} %get-tuple-element.106), channel_id=1, replica_groups=mesh['tm'=2,'cell'=16] {'cell'}, use_global_device_ids=true, to_apply=%region_13.14 | all-reduce | flops 256 | bytes 2048 | tf_op jit(solution)/shard_map/psum | solution.py:72
  227.8 29.5 %psum.119 = f32[2,128]{1,0:T(2,128)S(1)} all-reduce(f32[2,128]{1,0:T(2,128)S(1)} %get-tuple-element.108), channel_id=1, replica_groups=mesh['tm'=2,'cell'=16] {'cell'}, use_global_device_ids=true, to_apply=%region_15.16 | all-reduce | flops 256 | bytes 2048 | tf_op jit(solution)/shard_map/psum | solution.py:72
  258.3 4.4 collective-permute-start.1
  262.7 2.8 collective-permute-done.1
  265.8 29.5 %psum.120 = f32[2,128]{1,0:T(2,128)S(1)} all-reduce(f32[2,128]{1,0:T(2,128)S(1)} %fusion.8), channel_id=1, replica_groups=mesh['tm'=2,'cell'=16] {'cell'}, use_global_device_ids=true, to_apply=%region_17.18 | all-reduce | flops 256 | bytes 2048 | tf_op jit(solution)/shard_map/psum | solution.py:72
  296.2 29.5 %psum.121 = f32[2,128]{1,0:T(2,128)S(1)} all-reduce(f32[2,128]{1,0:T(2,128)S(1)} %get-tuple-element.63), channel_id=1, replica_groups=mesh['tm'=2,'cell'=16] {'cell'}, use_global_device_ids=true, to_apply=%region_19.20 | all-reduce | flops 256 | bytes 2048 | tf_op jit(solution)/shard_map/psum | solution.py:72
  326.2 29.5 %psum.122 = f32[2,128]{1,0:T(2,128)S(1)} all-reduce(f32[2,128]{1,0:T(2,128)S(1)} %get-tuple-element.111), channel_id=1, replica_groups=mesh['tm'=2,'cell'=16] {'cell'}, use_global_device_ids=true, to_apply=%region_21.22 | all-reduce | flops 256 | bytes 2048 | tf_op jit(solution)/shard_map/psum | solution.py:72
  356.3 29.5 %psum.123 = f32[2,128]{1,0:T(2,128)S(1)} all-reduce(f32[2,128]{1,0:T(2,128)S(1)} %get-tuple-element.53), channel_id=1, replica_groups=mesh['tm'=2,'cell'=16] {'cell'}, use_global_device_ids=true, to_apply=%region_23.24 | all-reduce | flops 256 | bytes 2048 | tf_op jit(solution)/shard_map/psum | solution.py:72
  386.4 29.5 %psum.124 = f32[2,128]{1,0:T(2,128)S(1)} all-reduce(f32[2,128]{1,0:T(2,128)S(1)} %get-tuple-element.114), channel_id=1, replica_groups=mesh['tm'=2,'cell'=16] {'cell'}, use_global_device_ids=true, to_apply=%region_25.26 | all-reduce | flops 256 | bytes 2048 | tf_op jit(solution)/shard_map/psum | solution.py:72
  416.0 0.4 fusion.51
  416.4 29.5 %psum.125 = f32[2,128]{1,0:T(2,128)S(1)} all-reduce(f32[2,128]{1,0:T(2,128)S(1)} %get-tuple-element.49), channel_id=1, replica_groups=mesh['tm'=2,'cell'=16] {'cell'}, use_global_device_ids=true, to_apply=%region_27.28 | all-reduce | flops 256 | bytes 2048 | tf_op jit(solution)/shard_map/psum | solution.py:72
  446.5 29.5 %psum.126 = f32[2,128]{1,0:T(2,128)S(1)} all-reduce(f32[2,128]{1,0:T(2,128)S(1)} %get-tuple-element.117), channel_id=1, replica_groups=mesh['tm'=2,'cell'=16] {'cell'}, use_global_device_ids=true, to_apply=%region_29.30 | all-reduce | flops 256 | bytes 2048 | tf_op jit(solution)/shard_map/psum | solution.py:72
  476.6 29.5 %psum.127 = f32[2,128]{1,0:T(2,128)S(1)} all-reduce(f32[2,128]{1,0:T(2,128)S(1)} %get-tuple-element.119), channel_id=1, replica_groups=mesh['tm'=2,'cell'=16] {'cell'}, use_global_device_ids=true, to_apply=%region_31.32 | all-reduce | flops 256 | bytes 2048 | tf_op jit(solution)/shard_map/psum | solution.py:72
  507.0 4.4 collective-permute-start.2
  511.5 2.7 collective-permute-done.2
  514.8 0.7 copy-done.8
  (88 shorter events, 12.1 us)
Async XLA Ops:
  0.0 47.0 %copy-start = (f32[2,2,128,128]{3,2,1,0:T(8,128)S(1)}, f32[2,2,128,128]{3,2,1,0:T(8,128)}, u32[]{:S(2)}) copy-start(f32[2,2,128,128]{3,2,1,0:T(8,128)} %param.9) | copy-start | bytes 786436
  1.5 0.7 copy-start.3
  1.5 1.0 copy-start.2
  2.8 0.9 copy-start.5
  3.7 0.9 slice-start
  4.6 7.6 %collective-permute-start = (f32[256,128]{1,0:T(8,128)S(1)}, f32[256,128]{1,0:T(8,128)S(1)}, u32[]{:S(2)}, u32[]{:S(2)}) collective-permute-start(f32[256,128]{1,0:T(8,128)S(1)} %fusion.13), channel_id=1, source_target_pairs={{0,16},{1,17},{2,18},{3,19},{4,20},{5,21},{6,22},{7,23},{8,24},{9,... | collective-permute-start | bytes 393224 | tf_op jit(solution)/shard_map/while/body/eval_jaxpr/ppermute | solution.py:13
  9.5 0.7 copy-start.7
  12.3 1.0 copy-start.4
  46.0 1.0 copy-start.1
  46.0 1.0 copy-start.6
  258.3 7.2 %collective-permute-start.1 = (f32[256,128]{1,0:T(8,128)S(1)}, f32[256,128]{1,0:T(8,128)S(1)}, u32[]{:S(2)}, u32[]{:S(2)}) collective-permute-start(f32[256,128]{1,0:T(8,128)S(1)} %fusion.11), channel_id=1, source_target_pairs={{0,16},{1,17},{2,18},{3,19},{4,20},{5,21},{6,22},{7,23},{8,24},{9,... | collective-permute-start | bytes 393224 | tf_op jit(solution)/shard_map/while/body/eval_jaxpr/ppermute | solution.py:13
  507.0 7.2 %collective-permute-start.2 = (f32[256,128]{1,0:T(8,128)S(1)}, f32[256,128]{1,0:T(8,128)S(1)}, u32[]{:S(2)}, u32[]{:S(2)}) collective-permute-start(f32[256,128]{1,0:T(8,128)S(1)} %fusion.12), channel_id=1, source_target_pairs={{0,16},{1,17},{2,18},{3,19},{4,20},{5,21},{6,22},{7,23},{8,24},{9,... | collective-permute-start | bytes 393224 | tf_op jit(solution)/shard_map/while/body/eval_jaxpr/ppermute | solution.py:13
  514.8 0.7 copy-start.8
where the time goes:
time: 516 us
  blocking collectives  475 us (92%)
  starting transfers between devices  13.7 us (3%)
  matrix products  11.5 us (2%)
  waiting for transfers between devices  7.54 us (1%)
    psum x16, blocking collectives, body(): average = lax.psum(jnp.sum(state, axis=1), 'cell') / total  475 us
    ppermute x3, starting transfers between devices, from_behind(): return lax.ppermute(block, axis, route)  13.7 us
  transfers between devices with their start and end apart: 3, of which 3 were waited for; matrix products, arithmetic and copies ran while one was open for 0% of the time, Pallas kernels for 0%

commit v1 on v0

--- a/solution.py
+++ b/solution.py
@@ -5,6 +5,11 @@
 
 FINE_MAX = 8
 ITERS = 2
+
+
+def add_all(value, name):
+    parts = lax.all_gather(value, name)
+    return jnp.sum(parts, axis=0)
 
 
 def from_behind(block, axis, distance):
@@ -69,7 +74,7 @@
         starts = jnp.concatenate([incoming[None], finals[:-1]], axis=0)
         state = starts
         for substep in range(FINE_MAX):
-            average = lax.psum(jnp.sum(state, axis=1), "cell") / total
+            average = add_all(jnp.sum(state, axis=1), "cell") / total
             moved = slices_mul(
                 state + source + mix_rate * (average[:, None, :] - state), fine_inverse
             )

time: 516 us -> 336 us (0.65)
  blocking collectives: 475 us -> 293 us
    psum x16 -> x0, blocking collectives: 475 us -> none  [body(): average = lax.psum(jnp.sum(state, axis=1), 'cell') / total]
    all_gather x0 -> x16, blocking collectives: none -> 293 us  [add_all(): parts = lax.all_gather(value, name)]
where the time goes in v1:
time: 336 us; the launch traced here: 335 us
  blocking collectives  293 us (87%)
  starting transfers between devices  13.7 us (4%)
  matrix products  11.5 us (3%)
  waiting for transfers between devices  8.5 us (3%)
  local copies, waits for them, and re-layouts  4.91 us (1%)
    all_gather x16, blocking collectives, add_all(): parts = lax.all_gather(value, name)  293 us
    ppermute x3, starting transfers between devices, from_behind(): return lax.ppermute(block, axis, route)  13.7 us
    dot_general x19, matrix products, slices_mul(): jnp.einsum('lgcs,lgst->lgct', shaped, matrices, precision=lax.Precision.H...  9.1 us
    ppermute x3, waiting for transfers between devices, from_behind(): return lax.ppermute(block, axis, route)  8.5 us
  transfers between devices with their start and end apart: 3, of which 3 were waited for; matrix products, arithmetic and copies ran while one was open for 0% of the time, Pallas kernels for 0%

profile of v1, /device:TPU:0, one launch (start us, length us, event | category | flops | bytes accessed | tf_op | source)
XLA Modules:
  0.0 335.2 jit_solution(12581406735547422280)
XLA Ops:
  0.0 1.5 fusion.61
  1.5 0.7 copy-done.3
  3.1 0.6 copy-done.5
  4.0 0.6 slice-done
  4.6 4.9 %collective-permute-start = (f32[256,128]{1,0:T(8,128)S(1)}, f32[256,128]{1,0:T(8,128)S(1)}, u32[]{:S(2)}, u32[]{:S(2)}) collective-permute-start(f32[256,128]{1,0:T(8,128)S(1)} %fusion.13), channel_id=1, source_target_pairs={{0,16},{1,17},{2,18},{3,19},{4,20},{5,21},{6,22},{7,23},{8,24},{9,... | collective-permute-start | bytes 393224 | tf_op jit(solution)/shard_map/while/body/eval_jaxpr/ppermute | solution.py:18
  9.5 0.7 copy-done.7
  10.2 2.0 collective-permute-done
  12.6 0.7 copy-done.4
  13.3 21.7 %all-gather.16 = f32[16,2,128]{2,1,0:T(2,128)S(1)} all-gather(f32[1,2,128]{2,1,0:T(2,128)S(1)} %bitcast.319), channel_id=2, replica_groups=mesh['tm'=2,'cell'=16] {'cell'}, dimensions={0}, use_global_device_ids=true | all-gather | bytes 17408 | tf_op jit(solution)/shard_map/all_gather | solution.py:11
  35.5 0.5 copy-done.1
  36.5 17.5 %all-gather.17 = f32[16,2,128]{2,1,0:T(2,128)S(1)} all-gather(f32[1,2,128]{2,1,0:T(2,128)S(1)} %bitcast.321), channel_id=3, replica_groups=mesh['tm'=2,'cell'=16] {'cell'}, dimensions={0}, use_global_device_ids=true | all-gather | bytes 17408 | tf_op jit(solution)/shard_map/all_gather | solution.py:11
  54.5 18.8 %all-gather.18 = f32[16,2,128]{2,1,0:T(2,128)S(1)} all-gather(f32[1,2,128]{2,1,0:T(2,128)S(1)} %bitcast.313), channel_id=4, replica_groups=mesh['tm'=2,'cell'=16] {'cell'}, dimensions={0}, use_global_device_ids=true | all-gather | bytes 17408 | tf_op jit(solution)/shard_map/all_gather | solution.py:11
  73.9 17.5 %all-gather.19 = f32[16,2,128]{2,1,0:T(2,128)S(1)} all-gather(f32[1,2,128]{2,1,0:T(2,128)S(1)} %bitcast.307), channel_id=5, replica_groups=mesh['tm'=2,'cell'=16] {'cell'}, dimensions={0}, use_global_device_ids=true | all-gather | bytes 17408 | tf_op jit(solution)/shard_map/all_gather | solution.py:11
  92.0 18.8 %all-gather.20 = f32[16,2,128]{2,1,0:T(2,128)S(1)} all-gather(f32[1,2,128]{2,1,0:T(2,128)S(1)} %bitcast.314), channel_id=6, replica_groups=mesh['tm'=2,'cell'=16] {'cell'}, dimensions={0}, use_global_device_ids=true | all-gather | bytes 17408 | tf_op jit(solution)/shard_map/all_gather | solution.py:11
  111.0 0.4 fusion.55
  111.4 17.5 %all-gather.21 = f32[16,2,128]{2,1,0:T(2,128)S(1)} all-gather(f32[1,2,128]{2,1,0:T(2,128)S(1)} %bitcast.308), channel_id=7, replica_groups=mesh['tm'=2,'cell'=16] {'cell'}, dimensions={0}, use_global_device_ids=true | all-gather | bytes 17408 | tf_op jit(solution)/shard_map/all_gather | solution.py:11
  129.5 18.8 %all-gather.22 = f32[16,2,128]{2,1,0:T(2,128)S(1)} all-gather(f32[1,2,128]{2,1,0:T(2,128)S(1)} %bitcast.315), channel_id=8, replica_groups=mesh['tm'=2,'cell'=16] {'cell'}, dimensions={0}, use_global_device_ids=true | all-gather | bytes 17408 | tf_op jit(solution)/shard_map/all_gather | solution.py:11
  148.9 17.5 %all-gather.23 = f32[16,2,128]{2,1,0:T(2,128)S(1)} all-gather(f32[1,2,128]{2,1,0:T(2,128)S(1)} %bitcast.311), channel_id=9, replica_groups=mesh['tm'=2,'cell'=16] {'cell'}, dimensions={0}, use_global_device_ids=true | all-gather | bytes 17408 | tf_op jit(solution)/shard_map/all_gather | solution.py:11
  167.4 4.4 %collective-permute-start.1 = (f32[256,128]{1,0:T(8,128)S(1)}, f32[256,128]{1,0:T(8,128)S(1)}, u32[]{:S(2)}, u32[]{:S(2)}) collective-permute-start(f32[256,128]{1,0:T(8,128)S(1)} %fusion.11), channel_id=1, source_target_pairs={{0,16},{1,17},{2,18},{3,19},{4,20},{5,21},{6,22},{7,23},{8,24},{9,... | collective-permute-start | bytes 393224 | tf_op jit(solution)/shard_map/while/body/eval_jaxpr/ppermute | solution.py:18
  171.8 3.2 collective-permute-done.1
  175.4 18.8 %all-gather.24 = f32[16,2,128]{2,1,0:T(2,128)S(1)} all-gather(f32[1,2,128]{2,1,0:T(2,128)S(1)} %bitcast.320), channel_id=10, replica_groups=mesh['tm'=2,'cell'=16] {'cell'}, dimensions={0}, use_global_device_ids=true | all-gather | bytes 17408 | tf_op jit(solution)/shard_map/all_gather | solution.py:11
  195.1 17.5 %all-gather.25 = f32[16,2,128]{2,1,0:T(2,128)S(1)} all-gather(f32[1,2,128]{2,1,0:T(2,128)S(1)} %bitcast.322), channel_id=11, replica_groups=mesh['tm'=2,'cell'=16] {'cell'}, dimensions={0}, use_global_device_ids=true | all-gather | bytes 17408 | tf_op jit(solution)/shard_map/all_gather | solution.py:11
  213.2 18.8 %all-gather.26 = f32[16,2,128]{2,1,0:T(2,128)S(1)} all-gather(f32[1,2,128]{2,1,0:T(2,128)S(1)} %bitcast.316), channel_id=12, replica_groups=mesh['tm'=2,'cell'=16] {'cell'}, dimensions={0}, use_global_device_ids=true | all-gather | bytes 17408 | tf_op jit(solution)/shard_map/all_gather | solution.py:11
  232.6 17.5 %all-gather.27 = f32[16,2,128]{2,1,0:T(2,128)S(1)} all-gather(f32[1,2,128]{2,1,0:T(2,128)S(1)} %bitcast.309), channel_id=13, replica_groups=mesh['tm'=2,'cell'=16] {'cell'}, dimensions={0}, use_global_device_ids=true | all-gather | bytes 17408 | tf_op jit(solution)/shard_map/all_gather | solution.py:11
  250.7 19.0 %all-gather.28 = f32[16,2,128]{2,1,0:T(2,128)S(1)} all-gather(f32[1,2,128]{2,1,0:T(2,128)S(1)} %bitcast.317), channel_id=14, replica_groups=mesh['tm'=2,'cell'=16] {'cell'}, dimensions={0}, use_global_device_ids=true | all-gather | bytes 17408 | tf_op jit(solution)/shard_map/all_gather | solution.py:11
  269.8 0.4 fusion.51
  270.2 17.5 %all-gather.29 = f32[16,2,128]{2,1,0:T(2,128)S(1)} all-gather(f32[1,2,128]{2,1,0:T(2,128)S(1)} %bitcast.310), channel_id=15, replica_groups=mesh['tm'=2,'cell'=16] {'cell'}, dimensions={0}, use_global_device_ids=true | all-gather | bytes 17408 | tf_op jit(solution)/shard_map/all_gather | solution.py:11
  288.3 18.8 %all-gather.30 = f32[16,2,128]{2,1,0:T(2,128)S(1)} all-gather(f32[1,2,128]{2,1,0:T(2,128)S(1)} %bitcast.318), channel_id=16, replica_groups=mesh['tm'=2,'cell'=16] {'cell'}, dimensions={0}, use_global_device_ids=true | all-gather | bytes 17408 | tf_op jit(solution)/shard_map/all_gather | solution.py:11
  307.7 17.5 %all-gather.31 = f32[16,2,128]{2,1,0:T(2,128)S(1)} all-gather(f32[1,2,128]{2,1,0:T(2,128)S(1)} %bitcast.312), channel_id=17, replica_groups=mesh['tm'=2,'cell'=16] {'cell'}, dimensions={0}, use_global_device_ids=true | all-gather | bytes 17408 | tf_op jit(solution)/shard_map/all_gather | solution.py:11
  326.2 4.4 %collective-permute-start.2 = (f32[256,128]{1,0:T(8,128)S(1)}, f32[256,128]{1,0:T(8,128)S(1)}, u32[]{:S(2)}, u32[]{:S(2)}) collective-permute-start(f32[256,128]{1,0:T(8,128)S(1)} %fusion.12), channel_id=1, source_target_pairs={{0,16},{1,17},{2,18},{3,19},{4,20},{5,21},{6,22},{7,23},{8,24},{9,... | collective-permute-start | bytes 393224 | tf_op jit(solution)/shard_map/while/body/eval_jaxpr/ppermute | solution.py:18
  330.6 3.2 collective-permute-done.2
  334.5 0.7 copy-done.8
  (104 shorter events, 12.5 us)
Async XLA Ops:
  0.0 36.0 %copy-start = (f32[2,2,128,128]{3,2,1,0:T(8,128)S(1)}, f32[2,2,128,128]{3,2,1,0:T(8,128)}, u32[]{:S(2)}) copy-start(f32[2,2,128,128]{3,2,1,0:T(8,128)} %param.9) | copy-start | bytes 786436
  1.5 0.7 copy-start.3
  1.5 1.0 copy-start.2
  2.8 0.9 copy-start.5
  3.7 0.9 slice-start
  4.6 7.6 %collective-permute-start = (f32[256,128]{1,0:T(8,128)S(1)}, f32[256,128]{1,0:T(8,128)S(1)}, u32[]{:S(2)}, u32[]{:S(2)}) collective-permute-start(f32[256,128]{1,0:T(8,128)S(1)} %fusion.13), channel_id=1, source_target_pairs={{0,16},{1,17},{2,18},{3,19},{4,20},{5,21},{6,22},{7,23},{8,24},{9,... | collective-permute-start | bytes 393224 | tf_op jit(solution)/shard_map/while/body/eval_jaxpr/ppermute | solution.py:18
  9.5 0.7 copy-start.7
  12.3 1.0 copy-start.4
  35.0 0.9 copy-start.1
  35.0 0.9 copy-start.6
  167.4 7.6 %collective-permute-start.1 = (f32[256,128]{1,0:T(8,128)S(1)}, f32[256,128]{1,0:T(8,128)S(1)}, u32[]{:S(2)}, u32[]{:S(2)}) collective-permute-start(f32[256,128]{1,0:T(8,128)S(1)} %fusion.11), channel_id=1, source_target_pairs={{0,16},{1,17},{2,18},{3,19},{4,20},{5,21},{6,22},{7,23},{8,24},{9,... | collective-permute-start | bytes 393224 | tf_op jit(solution)/shard_map/while/body/eval_jaxpr/ppermute | solution.py:18
  326.2 7.6 %collective-permute-start.2 = (f32[256,128]{1,0:T(8,128)S(1)}, f32[256,128]{1,0:T(8,128)S(1)}, u32[]{:S(2)}, u32[]{:S(2)}) collective-permute-start(f32[256,128]{1,0:T(8,128)S(1)} %fusion.12), channel_id=1, source_target_pairs={{0,16},{1,17},{2,18},{3,19},{4,20},{5,21},{6,22},{7,23},{8,24},{9,... | collective-permute-start | bytes 393224 | tf_op jit(solution)/shard_map/while/body/eval_jaxpr/ppermute | solution.py:18
  334.5 0.7 copy-start.8
